TPU v7x, 512 devices: a whole 4x4x16 slice. The times are simulated.
512 devices in a mesh: strata: 32 (over z, x_lo), shard: 16 (over y, x_hi, core).
Axes of the slice: x: 4 (x_hi: 2, x_lo: 2; x = x_hi * 2 + x_lo), y: 4, z: 16, core: 2. Of those that a mesh axis runs over, the one named last changes fastest.
Arguments:
- user_factors: bfloat16 [524288, 512], P(('strata', 'shard')), may hold values from -1.1953125 to 1.1953125
- item_factors: float32 [16384, 512], P(('strata', 'shard')), may hold values from -1.2 to 1.2
- tile_blocks: int32 [32, 16, 3, 8, 2], P('strata', 'shard'), may hold values from 0 to 7, as said below
- tile_counts: int32 [32, 16, 3], P('strata', 'shard'), may hold values from 1 to 8, as said below
- ratings: bfloat16 [32, 16, 3, 8, 128, 128], P('strata', 'shard'), may hold values from -5 to 5
- mask_words: int32 [32, 16, 3, 8, 16, 128], P('strata', 'shard'), may hold values from 0 to 255
Outputs:
- users_out: bfloat16 [524288, 512], P(('strata', 'shard'))
- items_out: float32 [16384, 512], P(('strata', 'shard'))
Inputs may be any that keep to these rules, and one draw needn't show every extreme that they name: `tile_blocks`: entry 0 is a user block below 8, entry 1 an item block below 4; the 8 pairs of one stratum, shard and visit are distinct. `tile_counts`: some stratum, shard and visit has exactly 8 live slots in every draw.
All inputs are finite; a program needn't handle non-finite values.
Results may differ from a plain program's by a relative error of at most 0.0095.
Values may be sent and summed in bfloat16 or wider, within the bound.
A program may use at most 64 MiB of HBM per device.

v0:
```python
import jax
import jax.numpy as jnp
from jax import lax
from jax.sharding import PartitionSpec as P

step_user = 0.05
step_item = 0.004
shrinkage = 0.05


def shifted(x, axis, by):
    peers = lax.axis_size(axis)
    return lax.ppermute(x, axis, [(i, (i + by) % peers) for i in range(peers)])


def unpack_mask(words):
    shifts = jnp.arange(8, dtype=jnp.int32)
    bits = jnp.bitwise_and(jnp.right_shift(words[:, :, None, :], shifts[None, None, :, None]), 1)
    return bits.reshape(words.shape[0], words.shape[1] * 8, words.shape[2]).astype(jnp.float32)


def device_terms(users, panel_low, blocks, count, rates, words):
    tile_side = rates.shape[-1]
    width = users.shape[1]
    user_count = users.shape[0] // tile_side
    item_count = panel_low.shape[0] // tile_side
    live = (jnp.arange(blocks.shape[0], dtype=jnp.int32) < count).astype(jnp.float32)
    weights = unpack_mask(words) * live[:, None, None]
    user_rows = jnp.take(users.reshape(user_count, tile_side, width), blocks[:, 0], axis=0)
    item_rows = jnp.take(panel_low.reshape(item_count, tile_side, width), blocks[:, 1], axis=0)
    predicted = jnp.einsum("kur,kir->kui", user_rows, item_rows, preferred_element_type=jnp.float32)
    error_tile = (weights * (rates.astype(jnp.float32) - predicted)).astype(jnp.bfloat16)
    user_terms = jnp.einsum(
        "kui,kir->kur", error_tile, item_rows, preferred_element_type=jnp.float32
    )
    item_terms = jnp.einsum(
        "kui,kur->kir", error_tile, user_rows, preferred_element_type=jnp.float32
    )
    user_hot = (blocks[:, 0][:, None] == jnp.arange(user_count, dtype=jnp.int32)[None, :]).astype(
        jnp.float32
    )
    item_hot = (blocks[:, 1][:, None] == jnp.arange(item_count, dtype=jnp.int32)[None, :]).astype(
        jnp.float32
    )
    grad_user = jnp.einsum(
        "kb,kur->bur", user_hot, user_terms, precision=lax.Precision.HIGHEST
    ).reshape(-1, width)
    grad_item = jnp.einsum(
        "kb,kir->bir", item_hot, item_terms, precision=lax.Precision.HIGHEST
    ).reshape(-1, width)
    return (grad_user, grad_item)


def shards(user_factors, item_factors, tile_blocks, tile_counts, ratings, mask_words):
    blocks_all = tile_blocks[0, 0]
    counts_all = tile_counts[0, 0]
    rates_all = ratings[0, 0]
    words_all = mask_words[0, 0]
    visits = counts_all.shape[0]
    users = user_factors
    panel = item_factors
    for visit in range(visits):
        panel_low = lax.all_gather(panel.astype(jnp.bfloat16), "shard", axis=0, tiled=True)
        grad_user, grad_item = device_terms(
            users,
            panel_low,
            blocks_all[visit],
            counts_all[visit],
            rates_all[visit],
            words_all[visit],
        )
        summed = lax.psum_scatter(
            grad_item.astype(jnp.bfloat16), "shard", scatter_dimension=0, tiled=True
        ).astype(jnp.float32)
        factor = users.astype(jnp.float32)
        users = (factor + step_user * (grad_user - shrinkage * factor)).astype(jnp.bfloat16)
        panel = panel + step_item * (summed - shrinkage * panel)
        if visit + 1 < visits:
            panel = shifted(panel.astype(jnp.bfloat16), "strata", 1).astype(panel.dtype)
    return (users, panel)


def solution(mesh):
    placed = (
        P(("strata", "shard"), None),
        P(("strata", "shard"), None),
        P("strata", "shard", None, None, None),
        P("strata", "shard", None),
        P("strata", "shard", None, None, None, None),
        P("strata", "shard", None, None, None, None),
    )
    return jax.shard_map(
        shards,
        mesh=mesh,
        in_specs=placed,
        out_specs=(P(("strata", "shard"), None), P(("strata", "shard"), None)),
        check_vma=False,
    )
```

profile of v0, /device:TPU:32, one launch (start us, length us, event | category | flops | bytes accessed | tf_op | source)
XLA Modules:
  0.0 393.6 jit_solution(7805216325913225970)
XLA Ops:
  13.2 1.5 slice_bitcast_fusion
  14.7 26.6 %all_gather.9 = bf16[512,512]{1,0:T(8,128)(2,1)S(1)} all-gather(bf16[32,512]{1,0:T(8,128)(2,1)S(1)} %convert_element_type.130), channel_id=1, replica_groups=mesh['strata'=32,'shard'=16] {'shard'}, dimensions={0}, use_global_device_ids=true | all-gather | bytes 557056 | tf_op jit(solution)/shard_map/all_gather | solution.py:63
  42.7 1.5 fusion.35
  44.8 2.2 fusion.21
  48.5 2.2 fusion.19
  52.5 83.5 %reduce-scatter.4.cloned.1.call-done = bf16[32,512]{1,0:T(8,128)(2,1)} async-done(((bf16[512,512]{1,0:T(8,128)(2,1)}), bf16[32,512]{1,0:T(8,128)(2,1)}) %reduce-scatter.4.cloned.1.call-update) | async-done | bytes 32784 | tf_op jit(solution)/shard_map/reduce_scatter | solution.py:72
  136.8 2.8 collective-permute-start
  140.2 1.6 gather_fusion.2
  141.8 1.7 collective-permute-done
  143.5 24.0 %all_gather.10 = bf16[512,512]{1,0:T(8,128)(2,1)S(1)} all-gather(bf16[32,512]{1,0:T(8,128)(2,1)S(1)} %collective-permute-done), channel_id=1, replica_groups=mesh['strata'=32,'shard'=16] {'shard'}, dimensions={0}, use_global_device_ids=true | all-gather | bytes 557056 | tf_op jit(solution)/shard_map/all_gather | solution.py:63
  168.1 1.9 fusion.34
  170.5 2.2 fusion.24
  174.9 2.2 fusion.15
  177.1 2.5 copy.10
  179.7 81.1 %reduce-scatter.6.cloned.1.call-done = bf16[32,512]{1,0:T(8,128)(2,1)} async-done(((bf16[512,512]{1,0:T(8,128)(2,1)}), bf16[32,512]{1,0:T(8,128)(2,1)}) %reduce-scatter.6.cloned.1.call-update) | async-done | bytes 32784 | tf_op jit(solution)/shard_map/reduce_scatter | solution.py:72
  261.5 2.8 collective-permute-start.1
  264.4 2.0 fusion.5
  266.4 1.6 gather_fusion.4
  268.3 24.7 %all_gather.11 = bf16[512,512]{1,0:T(8,128)(2,1)S(1)} all-gather(bf16[32,512]{1,0:T(8,128)(2,1)S(1)} %collective-permute-done.1), channel_id=1, replica_groups=mesh['strata'=32,'shard'=16] {'shard'}, dimensions={0}, use_global_device_ids=true | all-gather | bytes 557056 | tf_op jit(solution)/shard_map/all_gather | solution.py:63
  293.6 1.9 fusion.33
  296.0 2.2 fusion.27
  299.7 2.2 fusion.11
  303.1 1.4 fusion.8
  304.6 81.1 %reduce-scatter.8.cloned.1.call-done = bf16[32,512]{1,0:T(8,128)(2,1)} async-done(((bf16[512,512]{1,0:T(8,128)(2,1)}), bf16[32,512]{1,0:T(8,128)(2,1)}) %reduce-scatter.8.cloned.1.call-update) | async-done | bytes 32784 | tf_op jit(solution)/shard_map/reduce_scatter | solution.py:72
  (58 shorter events, 21.8 us)
Async XLA Ops:
  7.2 34.9 %copy-start.2 = (bf16[1024,512]{1,0:T(8,128)(2,1)S(1)}, bf16[1024,512]{1,0:T(8,128)(2,1)}, u32[]{:S(2)}) copy-start(bf16[1024,512]{1,0:T(8,128)(2,1)} %param.10) | copy-start | bytes 3145732
  7.2 128.8 %reduce-scatter.4.cloned.1.call-start = ((), (), s32[]{:S(2)}) async-start(), calls=%async_computation.3 | async-start | bytes 557056 | tf_op jit(solution)/shard_map/reduce_scatter | solution.py:72
  42.7 1.5 copy-start.5
  44.2 0.6 copy-start.6
  44.8 3.2 copy-start.4
  48.0 212.8 %reduce-scatter.6.cloned.1.call-start = ((), (), s32[]{:S(2)}) async-start(), calls=%async_computation.4 | async-start | bytes 557056 | tf_op jit(solution)/shard_map/reduce_scatter | solution.py:72
  52.0 84.0 %copy-start.3 = (f32[32,512]{1,0:T(8,128)S(1)}, f32[32,512]{1,0:T(8,128)}, u32[]{:S(2)}) copy-start(f32[32,512]{1,0:T(8,128)} %param.11) | copy-start | bytes 196612
  136.8 6.7 %collective-permute-start = (bf16[32,512]{1,0:T(8,128)(2,1)S(1)}, bf16[32,512]{1,0:T(8,128)(2,1)S(1)}, u32[]{:S(2)}, u32[]{:S(2)}) collective-permute-start(bf16[32,512]{1,0:T(8,128)(2,1)S(1)} %add_convert_fusion), channel_id=1, source_target_pairs={{0,16},{16,32},{32,48},{48,64},{64,80},{80,96},{96,112},{112,128},... | collective-permute-start | bytes 98312 | tf_op jit(solution)/shard_map/ppermute | solution.py:13
  140.2 27.9 %copy-start.7 = (s32[128]{0:T(128)S(1)}, s32[128]{0:T(128)}, u32[]{:S(2)}) copy-start(s32[128]{0:T(128)} %shift_right_arithmetic.70) | copy-start | bytes 1540
  168.1 1.9 copy-start.1
  173.7 212.0 %reduce-scatter.8.cloned.1.call-start = ((), (), s32[]{:S(2)}) async-start(), calls=%async_computation.5 | async-start | bytes 557056 | tf_op jit(solution)/shard_map/reduce_scatter | solution.py:72
  261.5 6.7 %collective-permute-start.1 = (bf16[32,512]{1,0:T(8,128)(2,1)S(1)}, bf16[32,512]{1,0:T(8,128)(2,1)S(1)}, u32[]{:S(2)}, u32[]{:S(2)}) collective-permute-start(bf16[32,512]{1,0:T(8,128)(2,1)S(1)} %fusion.53), channel_id=1, source_target_pairs={{0,16},{16,32},{32,48},{48,64},{64,80},{80,96},{96,112},{112,128},... | collective-permute-start | bytes 98312 | tf_op jit(solution)/shard_map/ppermute | solution.py:13
  293.6 1.9 copy-start
Sparse Core Ops, SparseCore 0:
  48.1 87.8 reduce-scatter.3
  173.8 86.9 reduce-scatter.5
  299.3 86.3 reduce-scatter.7
where the time goes:
time: 394 us
  waiting for transfers between devices  248 us (63%)
  blocking collectives  75.3 us (19%)
  matrix products  21.6 us (5%)
  local copies, waits for them, and re-layouts  18.3 us (5%)
  between operations  14.1 us (4%)
  other arithmetic  10.7 us (3%)
  starting transfers between devices  5.75 us (1%)
    reduce_scatter x3, waiting for transfers between devices, shards(): lax.psum_scatter(grad_item.astype(jnp.bfloat16), 'shard', scatter_dimensi...  246 us
    all_gather x3, blocking collectives, shards(): lax.all_gather(panel.astype(jnp.bfloat16), 'shard', axis=0, tiled=True)  75.3 us
  transfers between devices with their start and end apart: 5, of which 5 were waited for; matrix products, arithmetic and copies ran while one was open for 5% of the time, Pallas kernels for 0%

commit v1 on v0

--- a/solution.py
+++ b/solution.py
@@ -60,7 +60,10 @@
     users = user_factors
     panel = item_factors
     for visit in range(visits):
-        panel_low = lax.all_gather(panel.astype(jnp.bfloat16), "shard", axis=0, tiled=True)
+        state = panel.astype(jnp.bfloat16)
+        r_now = jnp.stack([state for _ in range(lax.axis_size("shard"))])
+        val2 = lax.all_to_all(r_now, "shard", 0, 0)
+        panel_low = jnp.concatenate(val2, 0)
         grad_user, grad_item = device_terms(
             users,
             panel_low,

time: 394 us -> 370 us (0.939)
  blocking collectives: 75.3 us -> 0 us
  waiting for transfers between devices: 248 us -> 283 us
  starting transfers between devices: 5.75 us -> 22.7 us
    all_gather x3 -> x0, blocking collectives: 75.3 us -> none  [shards(): lax.all_gather(panel.astype(jnp.bfloat16), 'shard', axis=0, tiled=True)]
    all_to_all x0 -> x3, waiting for transfers between devices: none -> 22.2 us  [shards(): val2 = lax.all_to_all(r_now, 'shard', 0, 0)]
    all_to_all x0 -> x3, starting transfers between devices: none -> 16.5 us  [shards(): val2 = lax.all_to_all(r_now, 'shard', 0, 0)]
    reduce_scatter x3, waiting for transfers between devices: 246 us -> 255 us  [shards(): lax.psum_scatter(grad_item.astype(jnp.bfloat16), 'shard', scatter_dimensi...]
  transfers between devices with their start and end apart: 5 -> 8, of which waited for: 5 -> 8; matrix products, arithmetic and copies ran while one was open for 5% -> 6% of each run, Pallas kernels for 0% -> 0%
where the time goes in v1:
time: 370 us; the launch traced here: 369 us
  waiting for transfers between devices  283 us (76%)
  starting transfers between devices  22.7 us (6%)
  matrix products  22.7 us (6%)
  local copies, waits for them, and re-layouts  17.5 us (5%)
  between operations  14.2 us (4%)
  other arithmetic  8.72 us (2%)
    reduce_scatter x3, waiting for transfers between devices, shards(): lax.psum_scatter(grad_item.astype(jnp.bfloat16), 'shard', scatter_dimensi...  255 us
    all_to_all x3, waiting for transfers between devices, shards(): val2 = lax.all_to_all(r_now, 'shard', 0, 0)  22.2 us
    all_to_all x3, starting transfers between devices, shards(): val2 = lax.all_to_all(r_now, 'shard', 0, 0)  16.5 us
  transfers between devices with their start and end apart: 8, of which 8 were waited for; matrix products, arithmetic and copies ran while one was open for 6% of the time, Pallas kernels for 0%

profile of v1, /device:TPU:32, one launch (start us, length us, event | category | flops | bytes accessed | tf_op | source)
XLA Modules:
  0.0 368.7 jit_solution(12400106865358108150)
XLA Ops:
  9.0 7.0 %all-to-all-start = ((bf16[16,32,512]{2,1,0:T(8,128)(2,1)}), bf16[16,32,512]{2,1,0:T(8,128)(2,1)S(1)}, u32[]{:S(2)}, u32[]{:S(2)}) async-start(bf16[16,32,512]{2,1,0:T(8,128)(2,1)} %stack.6), calls=%async_computation | async-start | bytes 1048576 | tf_op jit(solution)/shard_map/all_to_all | solution.py:65
  20.2 8.1 %all-to-all-done = bf16[16,32,512]{2,1,0:T(8,128)(2,1)S(1)} async-done(((bf16[16,32,512]{2,1,0:T(8,128)(2,1)}), bf16[16,32,512]{2,1,0:T(8,128)(2,1)S(1)}, u32[]{:S(2)}, u32[]{:S(2)}) %all-to-all-start) | async-done | bytes 524320 | tf_op jit(solution)/shard_map/all_to_all | solution.py:65
  31.0 2.2 fusion.21
  35.4 87.1 %reduce-scatter.4.cloned.1.call-done = bf16[32,512]{1,0:T(8,128)(2,1)} async-done(((bf16[512,512]{1,0:T(8,128)(2,1)}), bf16[32,512]{1,0:T(8,128)(2,1)}) %reduce-scatter.4.cloned.1.call-update) | async-done | bytes 32784 | tf_op jit(solution)/shard_map/reduce_scatter | solution.py:75
  123.3 2.8 collective-permute-start
  126.6 3.4 collective-permute-done
  130.8 4.7 %all-to-all-start.1 = ((bf16[16,32,512]{2,1,0:T(8,128)(2,1)}), bf16[16,32,512]{2,1,0:T(8,128)(2,1)S(1)}, u32[]{:S(2)}, u32[]{:S(2)}) async-start(bf16[16,32,512]{2,1,0:T(8,128)(2,1)} %stack.7), calls=%async_computation.2 | async-start | bytes 1048576 | tf_op jit(solution)/shard_map/all_to_all | solution.py:65
  135.8 2.2 fusion.19
  139.8 1.6 gather_fusion.2
  141.3 6.5 %all-to-all-done.1 = bf16[16,32,512]{2,1,0:T(8,128)(2,1)S(1)} async-done(((bf16[16,32,512]{2,1,0:T(8,128)(2,1)}), bf16[16,32,512]{2,1,0:T(8,128)(2,1)S(1)}, u32[]{:S(2)}, u32[]{:S(2)}) %all-to-all-start.1) | async-done | bytes 524320 | tf_op jit(solution)/shard_map/all_to_all | solution.py:65
  148.6 2.2 fusion.34
  151.3 2.2 fusion.24
  155.0 86.4 %reduce-scatter.6.cloned.1.call-done = bf16[32,512]{1,0:T(8,128)(2,1)} async-done(((bf16[512,512]{1,0:T(8,128)(2,1)}), bf16[32,512]{1,0:T(8,128)(2,1)}) %reduce-scatter.6.cloned.1.call-update) | async-done | bytes 32784 | tf_op jit(solution)/shard_map/reduce_scatter | solution.py:75
  242.2 2.8 collective-permute-start.1
  245.0 1.7 fusion.48
  246.7 2.2 collective-permute-done.1
  249.7 4.8 %all-to-all-start.2 = ((bf16[16,32,512]{2,1,0:T(8,128)(2,1)}), bf16[16,32,512]{2,1,0:T(8,128)(2,1)}, u32[]{:S(2)}, u32[]{:S(2)}) async-start(bf16[16,32,512]{2,1,0:T(8,128)(2,1)} %stack.8), calls=%async_computation.4 | async-start | bytes 1048576 | tf_op jit(solution)/shard_map/all_to_all | solution.py:65
  254.8 2.2 fusion.15
  259.3 7.6 %all-to-all-done.2 = bf16[16,32,512]{2,1,0:T(8,128)(2,1)} async-done(((bf16[16,32,512]{2,1,0:T(8,128)(2,1)}), bf16[16,32,512]{2,1,0:T(8,128)(2,1)}, u32[]{:S(2)}, u32[]{:S(2)}) %all-to-all-start.2) | async-done | bytes 524320 | tf_op jit(solution)/shard_map/all_to_all | solution.py:65
  266.9 1.7 gather_fusion.5
  268.6 1.5 fusion.33
  270.6 2.2 fusion.27
  274.2 2.2 fusion.11
  279.1 81.7 %reduce-scatter.8.cloned.1.call-done = bf16[32,512]{1,0:T(8,128)(2,1)} async-done(((bf16[512,512]{1,0:T(8,128)(2,1)}), bf16[32,512]{1,0:T(8,128)(2,1)}) %reduce-scatter.8.cloned.1.call-update) | async-done | bytes 32784 | tf_op jit(solution)/shard_map/reduce_scatter | solution.py:75
  (64 shorter events, 27.5 us)
Async XLA Ops:
  7.2 11.8 %copy-start.2 = (bf16[1024,512]{1,0:T(8,128)(2,1)S(1)}, bf16[1024,512]{1,0:T(8,128)(2,1)}, u32[]{:S(2)}) copy-start(bf16[1024,512]{1,0:T(8,128)(2,1)} %param.10) | copy-start | bytes 3145732
  7.2 12.4 %copy-start.5 = (s32[1,1,3,8,16,128]{5,4,3,2,1,0:T(8,128)S(1)}, s32[1,1,3,8,16,128]{5,4,3,2,1,0:T(8,128)}, u32[]{:S(2)}) copy-start(s32[1,1,3,8,16,128]{5,4,3,2,1,0:T(8,128)} %param.15) | copy-start | bytes 589828
  9.0 19.4 %all-to-all-start = ((bf16[16,32,512]{2,1,0:T(8,128)(2,1)}), bf16[16,32,512]{2,1,0:T(8,128)(2,1)S(1)}, u32[]{:S(2)}, u32[]{:S(2)}) async-start(bf16[16,32,512]{2,1,0:T(8,128)(2,1)} %stack.6), calls=%async_computation | async-start | bytes 1048576 | tf_op jit(solution)/shard_map/all_to_all | solution.py:65
  16.0 106.5 %reduce-scatter.4.cloned.1.call-start = ((), (), s32[]{:S(2)}) async-start(), calls=%async_computation.6 | async-start | bytes 557056 | tf_op jit(solution)/shard_map/reduce_scatter | solution.py:75
  31.0 91.5 %copy-start.4 = (f32[32,512]{1,0:T(8,128)S(1)}, f32[32,512]{1,0:T(8,128)}, u32[]{:S(2)}) copy-start(f32[32,512]{1,0:T(8,128)} %param.11) | copy-start | bytes 196612
  123.3 6.7 %collective-permute-start = (bf16[32,512]{1,0:T(8,128)(2,1)S(1)}, bf16[32,512]{1,0:T(8,128)(2,1)S(1)}, u32[]{:S(2)}, u32[]{:S(2)}) collective-permute-start(bf16[32,512]{1,0:T(8,128)(2,1)S(1)} %add_convert_fusion), channel_id=1, source_target_pairs={{0,16},{16,32},{32,48},{48,64},{64,80},{80,96},{96,112},{112,128},... | collective-permute-start | bytes 98312 | tf_op jit(solution)/shard_map/ppermute | solution.py:13
  130.8 17.0 %all-to-all-start.1 = ((bf16[16,32,512]{2,1,0:T(8,128)(2,1)}), bf16[16,32,512]{2,1,0:T(8,128)(2,1)S(1)}, u32[]{:S(2)}, u32[]{:S(2)}) async-start(bf16[16,32,512]{2,1,0:T(8,128)(2,1)} %stack.7), calls=%async_computation.2 | async-start | bytes 1048576 | tf_op jit(solution)/shard_map/all_to_all | solution.py:65
  135.6 105.9 %reduce-scatter.6.cloned.1.call-start = ((), (), s32[]{:S(2)}) async-start(), calls=%async_computation.7 | async-start | bytes 557056 | tf_op jit(solution)/shard_map/reduce_scatter | solution.py:75
  138.0 1.2 copy-start.3
  139.7 8.8 %copy-start.6 = (s32[8,16,128]{2,1,0:T(8,128)S(1)}, s32[8,16,128]{2,1,0:T(8,128)}, u32[]{:S(2)}) copy-start(s32[8,16,128]{2,1,0:T(8,128)} %get-tuple-element.18) | copy-start | bytes 196612
  139.7 8.8 %copy-start.7 = (f32[8]{0:T(128)S(1)}, f32[8]{0:T(128)}, u32[]{:S(2)}) copy-start(f32[8]{0:T(128)} %compare_convert_fusion.1) | copy-start | bytes 100
  148.5 5.9 %copy-start = (bf16[8,128,512]{2,1,0:T(8,128)(2,1)}, bf16[8,128,512]{2,1,0:T(8,128)(2,1)S(1)}, u32[]{:S(2)}) copy-start(bf16[8,128,512]{2,1,0:T(8,128)(2,1)S(1)} %gather_fusion.3) | copy-start | bytes 3145732
  148.5 2.2 copy-start.1
  242.2 6.7 %collective-permute-start.1 = (bf16[32,512]{1,0:T(8,128)(2,1)S(1)}, bf16[32,512]{1,0:T(8,128)(2,1)S(1)}, u32[]{:S(2)}, u32[]{:S(2)}) collective-permute-start(bf16[32,512]{1,0:T(8,128)(2,1)S(1)} %fusion.53), channel_id=1, source_target_pairs={{0,16},{16,32},{32,48},{48,64},{64,80},{80,96},{96,112},{112,128},... | collective-permute-start | bytes 98312 | tf_op jit(solution)/shard_map/ppermute | solution.py:13
  249.7 17.2 %all-to-all-start.2 = ((bf16[16,32,512]{2,1,0:T(8,128)(2,1)}), bf16[16,32,512]{2,1,0:T(8,128)(2,1)}, u32[]{:S(2)}, u32[]{:S(2)}) async-start(bf16[16,32,512]{2,1,0:T(8,128)(2,1)} %stack.8), calls=%async_computation.4 | async-start | bytes 1048576 | tf_op jit(solution)/shard_map/all_to_all | solution.py:65
  254.5 106.3 %reduce-scatter.8.cloned.1.call-start = ((), (), s32[]{:S(2)}) async-start(), calls=%async_computation.8 | async-start | bytes 557056 | tf_op jit(solution)/shard_map/reduce_scatter | solution.py:75
Sparse Core Ops, SparseCore 0:
  34.3 88.1 reduce-scatter.3
  154.5 86.8 reduce-scatter.5
  273.9 86.9 reduce-scatter.7
